TPU v7x, 32 devices: a whole 2x2x4 slice. The times are simulated.
32 devices in a mesh: ctx: 8 (over z, x), tp: 4 (over y, core).
Axes of the slice: x: 2, y: 2, z: 4, core: 2. Of those that a mesh axis runs over, the one named last changes fastest.
Arguments:
- queries: bfloat16 [1024, 8192], P('ctx', 'tp'), may hold values from -6 to 6
- keys: bfloat16 [4096, 1024], P(('ctx', 'tp')), may hold values from -6 to 6
- values: bfloat16 [4096, 1024], P(('ctx', 'tp')), may hold values from -6 to 6
- grad_out: bfloat16 [1024, 8192], P('ctx', 'tp'), may hold values from -6 to 6
- readers: int32 [8, 4], replicated, may hold values from -1 to 15, as said below
- token_mask: int32 [1024, 4], P('ctx'), may hold values from 0 to 1
- image_len: int32 [16], replicated, may hold values from 64 to 256
Outputs:
- grad_queries: bfloat16 [1024, 8192], P('ctx', 'tp')
- grad_keys: float32 [4096, 1024], P(('ctx', 'tp'))
- grad_values: float32 [4096, 1024], P(('ctx', 'tp'))
Inputs may be any that keep to these rules, and one draw needn't show every extreme that they name: `readers`: image m is owned by ctx index m // 2. Row c holds 2 runs of 2 consecutive slots; each run names 2 different images of one owner c - k, the first run with k = 0, the others with different k from 1 to 3; a run whose owner c - k is below 0 is all -1.
All inputs are finite; a program needn't handle non-finite values.
Results may differ from a plain program's by a relative error of at most 0.012.
Values may be sent and summed in bfloat16 or wider, within the bound.
A program may use at most 64 MiB of HBM per device.

v0:
```python
import functools

import jax
import jax.numpy as jnp
from jax import lax
from jax.experimental import pallas as pl
from jax.experimental.pallas import tpu as pltpu
from jax.sharding import PartitionSpec as P

HD = 128
IMG_DEV = 2
SLOTS = 4
WIN = 4
MESH = pl.DeviceIdType.MESH
NEG = -1e30
LOG2E = 1.4426950408889634


def kernel(
    n_ctx, n_tp, groups, per_group,
    readers, image_len, q, go, k, v, tm,
    gq, gk, gv,
    *scratch,
):
    nch = 2 * groups
    kvb = scratch[:nch]
    (bias, kcat, vcat, qs, gs, wt, dst, acc, prem, s1, sc, se, rp, rd, rc, fin, fout,
     loc_sem, a_send, a_recv, f_send, f_recv, b_send, b_recv, z_send, z_recv) = scratch[nch:]
    rows = k.shape[0]
    half = rows * n_tp
    itok = half // IMG_DEV
    toks = q.shape[0]
    scaling = HD ** (-0.5)
    c = lax.axis_index("ctx")
    t = lax.axis_index("tp")
    even = lax.rem(c, 2) == 0
    odd = lax.rem(c, 2) == 1
    partner = c + 1 - 2 * lax.rem(c, 2)
    has_up = c + 2 < n_ctx
    has_down = c >= 2

    barrier = pltpu.get_barrier_semaphore()
    for d in range(1, n_tp):
        pl.semaphore_signal(barrier, inc=1, device_id=(c, lax.rem(t + d, n_tp)), device_id_type=MESH)
    pl.semaphore_signal(barrier, inc=1, device_id=(partner, t), device_id_type=MESH)

    @pl.when(has_up)
    def _():
        pl.semaphore_signal(barrier, inc=1, device_id=(c + 2, t), device_id_type=MESH)

    @pl.when(has_down)
    def _():
        pl.semaphore_signal(barrier, inc=1, device_id=(c - 2, t), device_id_type=MESH)

    both = has_up & has_down

    @pl.when(both)
    def _():
        pl.semaphore_wait(barrier, n_tp + 2)

    @pl.when(jnp.logical_not(both))
    def _():
        pl.semaphore_wait(barrier, n_tp + 1)

    def copy(src, dst_ref, send, recv, ctx, tp):
        return pltpu.make_async_remote_copy(
            src_ref=src, dst_ref=dst_ref, send_sem=send, recv_sem=recv,
            device_id=(ctx, tp), device_id_type=MESH,
        )

    def gather(ch, d):
        src = (k, v)[ch % 2]
        to = lax.rem(t + d, n_tp)
        cols = pl.ds(pl.multiple_of((to * groups + ch // 2) * HD, HD), HD)
        return copy(
            src.at[:, cols], kvb[ch].at[0, pl.ds(pl.multiple_of(t * rows, rows), rows)],
            a_send.at[d - 1, ch], a_recv.at[d - 1, ch], c, to,
        )

    def gather_own(ch):
        src = (k, v)[ch % 2]
        cols = pl.ds(pl.multiple_of((t * groups + ch // 2) * HD, HD), HD)
        return pltpu.make_async_copy(
            src.at[:, cols], kvb[ch].at[0, pl.ds(pl.multiple_of(t * rows, rows), rows)],
            loc_sem.at[ch],
        )

    for ch in range(nch):
        for d in range(1, n_tp):
            gather(ch, d).start()
        gather_own(ch).start()

    rem_id = readers[c, IMG_DEV]
    rem_ok = rem_id >= 0
    rem_owner = jnp.maximum(rem_id, 0) // IMG_DEV
    ksel = jnp.where(rem_ok, c - rem_owner, 0)
    kload = jnp.clip(ksel, 0, WIN - 1)
    up_row = jnp.minimum(c + 1, n_ctx - 1)
    up_id = readers[up_row, IMG_DEV]
    up_k = jnp.where(up_id >= 0, c + 1 - jnp.maximum(up_id, 0) // IMG_DEV, 0)
    for b in range(SLOTS):
        run = (b // IMG_DEV) * IMG_DEV
        owner = c if b < IMG_DEV else rem_owner
        image = owner * IMG_DEV + b % IMG_DEV
        length = image_len[image]
        if b >= IMG_DEV:
            length = jnp.where(rem_ok, length, 0)
        mask = jnp.where(readers[c, run] == image, tm[run : run + 1], tm[run + 1 : run + 2])
        live = jnp.where(mask == 1, length, 0)
        place = lax.broadcasted_iota(jnp.int32, (itok, toks), 0)
        block = jnp.where(place < live, 0.0, NEG).astype(jnp.float32)
        bias[pl.ds(b * itok, itok), :toks] = block
        bias[pl.ds(b * itok, itok), toks:] = block

    def own_next(ch):
        return copy(kvb[ch].at[0], kvb[ch].at[1], f_send.at[0, ch], f_recv.at[0, ch], partner, t)

    def own_up(ch):
        return copy(kvb[ch].at[0], kvb[ch].at[2], f_send.at[1, ch], f_recv.at[1, ch], c + 2, t)

    def two_back(ch):
        return copy(kvb[ch].at[2], kvb[ch].at[1], f_send.at[0, ch], f_recv.at[0, ch], partner, t)

    def one_up(ch):
        return copy(kvb[ch].at[1], kvb[ch].at[3], f_send.at[2, ch], f_recv.at[2, ch], c + 2, t)

    def two_next(ch):
        return copy(kvb[ch].at[2], kvb[ch].at[3], f_send.at[3, ch], f_recv.at[2, ch], partner, t)

    for ch in range(nch):
        for d in range(1, n_tp):
            gather(ch, d).wait_recv()
        gather_own(ch).wait()

        @pl.when(has_up)
        def _():
            own_up(ch).start()

        @pl.when(even)
        def _():
            own_next(ch).start()

    for ch in range(nch):
        @pl.when(has_down)
        def _():
            own_up(ch).wait_recv()

            @pl.when(even)
            def _():
                two_next(ch).start()

            @pl.when(odd)
            def _():
                two_back(ch).start()

        @pl.when(even & has_down)
        def _():
            two_back(ch).wait_recv()

            @pl.when(has_up)
            def _():
                one_up(ch).start()

        @pl.when(odd)
        def _():
            own_next(ch).wait_recv()

    def arrive(ch):
        @pl.when(odd & has_down)
        def _():
            two_next(ch).wait_recv()

        @pl.when(even & (c >= 4))
        def _():
            one_up(ch).wait_recv()

    def first_send(ch):
        @pl.when(odd)
        def _():
            copy(s1.at[ch], rp.at[ch], b_send.at[0, ch], b_recv.at[0, ch], partner, t).start()

        @pl.when(even & has_down)
        def _():
            copy(s1.at[ch], rd.at[ch], b_send.at[0, ch], b_recv.at[1, ch], c - 2, t).start()

    send_partial = jnp.where(odd, ((ksel == 1) | (ksel == 3)), ksel == 3)

    for g in range(groups):
        for ch in (2 * g, 2 * g + 1):
            arrive(ch)
        kcat[:half] = kvb[2 * g][0]
        kcat[half:] = kvb[2 * g][kload]
        vcat[:half] = kvb[2 * g + 1][0]
        vcat[half:] = kvb[2 * g + 1][kload]
        for h in range(per_group):
            cols = pl.ds((g * per_group + h) * HD, HD)
            qs[pl.ds(h * toks, toks)] = q[:, cols]
            gs[pl.ds(h * toks, toks)] = go[:, cols]
        kt = jnp.transpose(kcat[...])

        def pair_step(p, carry):
            span = pl.ds(pl.multiple_of(p * 2 * toks, 2 * toks), 2 * toks)
            nt = (((1,), (1,)), ((), ()))
            score = lax.dot_general(kcat[...], qs[span], nt, preferred_element_type=jnp.float32)
            x = score * (scaling * LOG2E) + bias[...]
            top = jnp.maximum(jnp.max(x, axis=0, keepdims=True), 0.1 * NEG)
            e = jnp.exp2(x - top)
            inv = 1.0 / jnp.maximum(jnp.sum(e, axis=0, keepdims=True), 1.0)
            w = e * inv
            wt[:, span] = w.astype(jnp.bfloat16)
            gw = lax.dot_general(vcat[...], gs[span], nt, preferred_element_type=jnp.float32)
            u = w * gw
            dot = jnp.sum(u, axis=0, keepdims=True)
            ds = (u - w * dot).astype(jnp.bfloat16)
            dst[:, span] = ds
            gqt = jnp.dot(kt, ds, preferred_element_type=jnp.float32) * scaling
            for i in range(2):
                cols = pl.ds(pl.multiple_of((g * per_group + 2 * p + i) * HD, HD), HD)
                gq[:, cols] = jnp.transpose(gqt[:, i * toks : (i + 1) * toks]).astype(jnp.bfloat16)
            return carry

        lax.fori_loop(0, per_group // 2, pair_step, 0)
        for ch, (lhs, rhs) in ((2 * g, (dst, qs)), (2 * g + 1, (wt, gs))):
            scale = scaling if ch % 2 == 0 else 1.0
            total = jnp.dot(lhs[...], rhs[...], preferred_element_type=jnp.float32) * scale
            acc[ch] = total[:half]
            part = jnp.where(rem_ok, total[half:], 0.0).astype(jnp.bfloat16)
            prem[ch] = part
            s1[ch] = jnp.where(send_partial, part, jnp.zeros_like(part))
            first_send(ch)

    def from_partner(ch):
        return copy(s1.at[ch], rp.at[ch], b_send.at[0, ch], b_recv.at[0, ch], partner, t)

    def three_down(ch):
        return copy(s1.at[ch], rd.at[ch], b_send.at[0, ch], b_recv.at[1, ch], c - 2, t)

    def two_down(ch):
        return copy(sc.at[ch], rc.at[ch], b_send.at[1, ch], b_recv.at[2, ch], c - 2, t)

    def one_next(ch):
        return copy(se.at[ch], rp.at[ch], b_send.at[2, ch], b_recv.at[0, ch], partner, t)

    def picked(ch, cond):
        part = prem[ch]
        return jnp.where(cond, part, jnp.zeros_like(part)).astype(jnp.float32)

    for ch in range(nch):
        @pl.when(even)
        def _():
            from_partner(ch).wait_recv()
            got = rp[ch].astype(jnp.float32)
            acc[ch] = acc[ch] + jnp.where(up_k == 1, got, 0.0)

            @pl.when(has_down)
            def _():
                sc[ch] = (picked(ch, ksel == 2) + jnp.where(up_k == 3, got, 0.0)).astype(jnp.bfloat16)
                two_down(ch).start()

        @pl.when(even & has_up)
        def _():
            three_down(ch).wait_recv()

        @pl.when(even & has_down & has_up)
        def _():
            se[ch] = (picked(ch, ksel == 1) + rd[ch].astype(jnp.float32)).astype(jnp.bfloat16)
            one_next(ch).start()

        @pl.when(even & has_down & (c + 2 >= n_ctx))
        def _():
            se[ch] = picked(ch, ksel == 1).astype(jnp.bfloat16)
            one_next(ch).start()

    def hand(ch, d):
        to = lax.rem(t + d, n_tp)
        return copy(
            fout.at[ch, pl.ds(pl.multiple_of(to * rows, rows), rows)], fin.at[d - 1, ch],
            z_send.at[d - 1, ch], z_recv.at[d - 1, ch], c, to,
        )

    for ch in range(nch):
        @pl.when(odd & has_down)
        def _():
            one_next(ch).wait_recv()
            sc[ch] = (picked(ch, ksel == 2) + rp[ch].astype(jnp.float32)).astype(jnp.bfloat16)
            two_down(ch).start()

    for ch in range(nch):
        @pl.when(has_up)
        def _():
            two_down(ch).wait_recv()
            acc[ch] = acc[ch] + rc[ch].astype(jnp.float32)

        fout[ch] = acc[ch].astype(jnp.bfloat16)
        for d in range(1, n_tp):
            hand(ch, d).start()

    def put(ch, who, block):
        out = (gk, gv)[ch % 2]
        out[:, pl.ds(pl.multiple_of((who * groups + ch // 2) * HD, HD), HD)] = block

    for ch in range(nch):
        put(ch, t, acc[ch, pl.ds(pl.multiple_of(t * rows, rows), rows)])
    for ch in range(nch):
        for d in range(1, n_tp):
            hand(ch, d).wait_recv()
            put(ch, lax.rem(t + n_tp - d, n_tp), fin[d - 1, ch].astype(jnp.float32))

    for ch in range(nch):
        for d in range(1, n_tp):
            gather(ch, d).wait_send()
            hand(ch, d).wait_send()

        @pl.when(has_up)
        def _():
            own_up(ch).wait_send()

        @pl.when(even)
        def _():
            own_next(ch).wait_send()

        @pl.when(odd)
        def _():
            from_partner(ch).wait_send()

        @pl.when(odd & has_down)
        def _():
            two_back(ch).wait_send()

        @pl.when(even & has_down)
        def _():
            two_next(ch).wait_send()
            three_down(ch).wait_send()
            one_next(ch).wait_send()

        @pl.when(even & has_down & has_up)
        def _():
            one_up(ch).wait_send()

        @pl.when(has_down)
        def _():
            two_down(ch).wait_send()


def on_device(n_ctx, n_tp, queries, keys, values, grad_out, readers, token_mask, image_len):
    rows, width = keys.shape
    groups = width // HD // n_tp
    toks = queries.shape[0]
    per_group = queries.shape[1] // HD // groups
    nch = 2 * groups
    half = rows * n_tp
    bf, f32 = jnp.bfloat16, jnp.float32
    vm = pl.BlockSpec(memory_space=pltpu.VMEM)
    sm = pl.BlockSpec(memory_space=pltpu.SMEM)
    dma = pltpu.SemaphoreType.DMA
    item = pltpu.VMEM((nch, half, HD), bf)
    return pl.pallas_call(
        functools.partial(kernel, n_ctx, n_tp, groups, per_group),
        out_shape=(
            jax.ShapeDtypeStruct(queries.shape, bf),
            jax.ShapeDtypeStruct(keys.shape, f32),
            jax.ShapeDtypeStruct(keys.shape, f32),
        ),
        in_specs=[sm, sm, vm, vm, vm, vm, vm],
        out_specs=(vm, vm, vm),
        scratch_shapes=[pltpu.VMEM((WIN, half, HD), bf)] * nch
        + [
            pltpu.VMEM((2 * half, 2 * toks), f32),
            pltpu.VMEM((2 * half, HD), bf),
            pltpu.VMEM((2 * half, HD), bf),
            pltpu.VMEM((per_group * toks, HD), bf),
            pltpu.VMEM((per_group * toks, HD), bf),
            pltpu.VMEM((2 * half, per_group * toks), bf),
            pltpu.VMEM((2 * half, per_group * toks), bf),
            pltpu.VMEM((nch, half, HD), f32),
            item, item, item, item, item, item, item,
            pltpu.VMEM((n_tp - 1, nch, rows, HD), bf),
            item,
            dma((nch,)),
            dma((n_tp - 1, nch)), dma((n_tp - 1, nch)),
            dma((4, nch)), dma((3, nch)),
            dma((3, nch)), dma((3, nch)),
            dma((n_tp - 1, nch)), dma((n_tp - 1, nch)),
        ],
        compiler_params=pltpu.CompilerParams(
            collective_id=0, has_side_effects=True, vmem_limit_bytes=50 * 1024 * 1024
        ),
    )(readers, image_len, queries, grad_out, keys, values, token_mask.T)


def solution(mesh):
    n_ctx, n_tp = mesh.shape["ctx"], mesh.shape["tp"]
    return jax.shard_map(
        functools.partial(on_device, n_ctx, n_tp),
        mesh=mesh,
        in_specs=(
            P("ctx", "tp"),
            P(("ctx", "tp"), None),
            P(("ctx", "tp"), None),
            P("ctx", "tp"),
            P(),
            P("ctx", None),
            P(),
        ),
        out_specs=(P("ctx", "tp"), P(("ctx", "tp"), None), P(("ctx", "tp"), None)),
        check_vma=False,
    )
```

profile of v0, /device:TPU:15, one launch (start us, length us, event | category | flops | bytes accessed | tf_op | source)
XLA Modules:
  0.0 70.8 jit_solution(7335798550747034954)
XLA Ops:
  0.6 0.0 copy-start.4
  0.6 0.0 copy-start.5
  0.7 0.8 %copy.10.readers = s32[8,4]{1,0:T(8,128)S(1)} copy(s32[8,4]{0,1:T(4,128)} %param.11) | data formatting | bytes 256 | tf_op args[4]
  1.4 0.0 copy-done.4
  1.4 0.0 copy-done.5
  1.4 0.0 copy-start
  1.4 1.0 %copy-done = bf16[128,2048]{1,0:T(8,128)(2,1)S(1)} copy-done((bf16[128,2048]{1,0:T(8,128)(2,1)S(1)}, bf16[128,2048]{1,0:T(8,128)(2,1)}, u32[]{:S(2)}) %copy-start) | copy-done | bytes 524312
  2.5 0.0 copy-start.1
  2.5 1.0 %copy-done.1 = bf16[128,2048]{1,0:T(8,128)(2,1)S(1)} copy-done((bf16[128,2048]{1,0:T(8,128)(2,1)S(1)}, bf16[128,2048]{1,0:T(8,128)(2,1)}, u32[]{:S(2)}) %copy-start.1) | copy-done | bytes 524312
  3.5 0.0 copy-start.2
  3.5 0.9 %copy-done.2 = bf16[128,1024]{1,0:T(8,128)(2,1)S(1)} copy-done((bf16[128,1024]{1,0:T(8,128)(2,1)S(1)}, bf16[128,1024]{1,0:T(8,128)(2,1)}, u32[]{:S(2)}) %copy-start.2) | copy-done | bytes 262168
  4.5 0.0 copy-start.3
  4.5 0.9 %copy-done.3 = bf16[128,1024]{1,0:T(8,128)(2,1)S(1)} copy-done((bf16[128,1024]{1,0:T(8,128)(2,1)S(1)}, bf16[128,1024]{1,0:T(8,128)(2,1)}, u32[]{:S(2)}) %copy-start.3) | copy-done | bytes 262168
  5.4 63.0 %shard_map.94 = (bf16[128,2048]{1,0:T(8,128)(2,1)S(1)}, f32[128,1024]{1,0:T(8,128)S(1)}, f32[128,1024]{1,0:T(8,128)S(1)}) custom-call(s32[8,4]{1,0:T(8,128)S(1)} %copy.10.readers, s32[16]{0:T(128)S(1)} %copy-done.5, bf16[128,2048]{1,0:T(8,128)(2,1)S(1)} %copy-done, bf16[128,2048]{1,0:T(8,128)(2,1)S(1)} %copy-done.1, bf16[128,1024]{1,0:T(8,128)(2,1)S(1)} %copy-done.2, ...), custom_call_target="tpu_custom_call" | custom-call | tf_op jit(solution)/shard_map/pallas_call | solution.py:357
  68.5 0.8 %copy.14 = bf16[128,2048]{1,0:T(8,128)(2,1)} copy(bf16[128,2048]{1,0:T(8,128)(2,1)S(1)} %get-tuple-element.6) | data formatting | bytes 1048576
  69.3 0.8 %copy.15 = f32[128,1024]{1,0:T(8,128)} copy(f32[128,1024]{1,0:T(8,128)S(1)} %get-tuple-element.7) | data formatting | bytes 1048576
  70.0 0.8 %copy.16 = f32[128,1024]{1,0:T(8,128)} copy(f32[128,1024]{1,0:T(8,128)S(1)} %get-tuple-element.8) | data formatting | bytes 1048576
Async XLA Ops:
  0.6 0.8 %copy-start.4 = (s32[128,4]{0,1:T(4,128)S(1)}, s32[128,4]{0,1:T(4,128)}, u32[]{:S(2)}) copy-start(s32[128,4]{0,1:T(4,128)} %param.12) | copy-start | bytes 6148
  0.6 0.8 %copy-start.5 = (s32[16]{0:T(128)S(1)}, s32[16]{0:T(128)}, u32[]{:S(2)}) copy-start(s32[16]{0:T(128)} %image_len.1) | copy-start | bytes 196
  1.4 1.0 %copy-start = (bf16[128,2048]{1,0:T(8,128)(2,1)S(1)}, bf16[128,2048]{1,0:T(8,128)(2,1)}, u32[]{:S(2)}) copy-start(bf16[128,2048]{1,0:T(8,128)(2,1)} %q.1) | copy-start | bytes 1572868
  2.5 1.0 %copy-start.1 = (bf16[128,2048]{1,0:T(8,128)(2,1)S(1)}, bf16[128,2048]{1,0:T(8,128)(2,1)}, u32[]{:S(2)}) copy-start(bf16[128,2048]{1,0:T(8,128)(2,1)} %go.1) | copy-start | bytes 1572868
  3.5 0.9 %copy-start.2 = (bf16[128,1024]{1,0:T(8,128)(2,1)S(1)}, bf16[128,1024]{1,0:T(8,128)(2,1)}, u32[]{:S(2)}) copy-start(bf16[128,1024]{1,0:T(8,128)(2,1)} %k.1) | copy-start | bytes 786436
  4.5 0.9 %copy-start.3 = (bf16[128,1024]{1,0:T(8,128)(2,1)S(1)}, bf16[128,1024]{1,0:T(8,128)(2,1)}, u32[]{:S(2)}) copy-start(bf16[128,1024]{1,0:T(8,128)(2,1)} %v.1) | copy-start | bytes 786436
where the time goes:
time: 71.2 us; the launch traced here: 70.8 us
  Pallas kernels  63 us (88%)
  local copies, waits for them, and re-layouts  7.14 us (10%)
    pallas_call x1, Pallas kernels, on_device(): pl.pallas_call(functools.partial(kernel, n_ctx, n_tp, groups, per_group),...  63 us
    unnamed x16, local copies, waits for them, and re-layouts  7.14 us

commit v1 on v0

v1 whole, which is shorter than its diff:
```python
import functools

import jax
import jax.numpy as jnp
from jax import lax
from jax.experimental import pallas as pl
from jax.experimental.pallas import tpu as pltpu
from jax.sharding import PartitionSpec as P

HD = 128
IMG_DEV = 2
SLOTS = 4
WIN = 4
MESH = pl.DeviceIdType.MESH
NEG = -1e30
LOG2E = 1.4426950408889634


def kernel(
    n_ctx, n_tp, groups, per_group,
    readers, image_len, q, go, k, v, tm,
    gq, gk, gv,
    *scratch,
):
    nch = 2 * groups
    kvb = scratch[:nch]
    (bias, kcat, vcat, qs, gs, wt, dst, acc, prem, s1, sc, se, rp, rd, rc, fin, fout, st,
     q_sem, loc_sem, a_send, a_recv, f_send, f_recv, b_send, b_recv, z_send, z_recv) = scratch[nch:]
    rows = k.shape[0]
    half = rows * n_tp
    itok = half // IMG_DEV
    toks = q.shape[0]
    scaling = HD ** (-0.5)
    c = lax.axis_index("ctx")
    t = lax.axis_index("tp")
    even = lax.rem(c, 2) == 0
    odd = lax.rem(c, 2) == 1
    partner = c + 1 - 2 * lax.rem(c, 2)
    has_up = c + 2 < n_ctx
    has_down = c >= 2

    barrier = pltpu.get_barrier_semaphore()
    for d in range(1, n_tp):
        pl.semaphore_signal(barrier, inc=1, device_id=(c, lax.rem(t + d, n_tp)), device_id_type=MESH)
    pl.semaphore_signal(barrier, inc=1, device_id=(partner, t), device_id_type=MESH)

    @pl.when(has_up)
    def _():
        pl.semaphore_signal(barrier, inc=1, device_id=(c + 2, t), device_id_type=MESH)

    @pl.when(has_down)
    def _():
        pl.semaphore_signal(barrier, inc=1, device_id=(c - 2, t), device_id_type=MESH)

    both = has_up & has_down

    @pl.when(both)
    def _():
        pl.semaphore_wait(barrier, n_tp + 2)

    @pl.when(jnp.logical_not(both))
    def _():
        pl.semaphore_wait(barrier, n_tp + 1)

    def copy(src, dst_ref, send, recv, ctx, tp):
        return pltpu.make_async_remote_copy(
            src_ref=src, dst_ref=dst_ref, send_sem=send, recv_sem=recv,
            device_id=(ctx, tp), device_id_type=MESH,
        )

    def gather(ch, d):
        src = (k, v)[ch % 2]
        to = lax.rem(t + d, n_tp)
        cols = pl.ds(pl.multiple_of((to * groups + ch // 2) * HD, HD), HD)
        return copy(
            src.at[:, cols], kvb[ch].at[0, pl.ds(pl.multiple_of(t * rows, rows), rows)],
            a_send.at[d - 1, ch], a_recv.at[d - 1, ch], c, to,
        )

    def gather_own(ch):
        src = (k, v)[ch % 2]
        cols = pl.ds(pl.multiple_of((t * groups + ch // 2) * HD, HD), HD)
        return pltpu.make_async_copy(
            src.at[:, cols], kvb[ch].at[0, pl.ds(pl.multiple_of(t * rows, rows), rows)],
            loc_sem.at[ch],
        )

    for ch in range(nch):
        for d in range(1, n_tp):
            gather(ch, d).start()
        gather_own(ch).start()

    def head_copy(which, h):
        src, into = ((q, qs), (go, gs))[which]
        return pltpu.make_async_copy(
            src.at[:, pl.ds(h * HD, HD)], into.at[pl.ds(h * toks, toks)], q_sem.at[which, h]
        )

    for h in range(groups * per_group):
        head_copy(0, h).start()
        head_copy(1, h).start()

    rem_id = readers[IMG_DEV, c]
    rem_ok = rem_id >= 0
    rem_owner = jnp.maximum(rem_id, 0) // IMG_DEV
    ksel = jnp.where(rem_ok, c - rem_owner, 0)
    near = jnp.where(ksel == 2, 2, jnp.where(ksel == 0, 0, 1))
    slot_of = (jnp.where(even & (ksel == 3), 3, near), near)
    side_id = readers[IMG_DEV, partner]
    side_k = jnp.where(side_id >= 0, partner - jnp.maximum(side_id, 0) // IMG_DEV, 0)
    for b in range(SLOTS):
        run = (b // IMG_DEV) * IMG_DEV
        owner = c if b < IMG_DEV else rem_owner
        image = owner * IMG_DEV + b % IMG_DEV
        length = image_len[image]
        if b >= IMG_DEV:
            length = jnp.where(rem_ok, length, 0)
        mask = jnp.where(readers[run, c] == image, tm[run : run + 1], tm[run + 1 : run + 2])
        live = jnp.where(mask == 1, length, 0)
        place = lax.broadcasted_iota(jnp.int32, (itok, toks), 0)
        block = jnp.where(place < live, 0.0, NEG).astype(jnp.float32)
        bias[pl.ds(b * itok, itok), :toks] = block
        bias[pl.ds(b * itok, itok), toks:] = block

    def own_up(ch):
        return copy(kvb[ch].at[0], kvb[ch].at[2], f_send.at[0, ch], f_recv.at[0, ch], c + 2, t)

    def side(ch, src):
        return copy(src, kvb[ch].at[1], f_send.at[1, ch], f_recv.at[1, ch], partner, t)

    def relay(ch):
        src = kvb[ch].at[1 + ch % 2]
        return copy(src, kvb[ch].at[3], f_send.at[2, ch], f_recv.at[2, ch], c + 2, t)

    for ch in range(nch):
        for d in range(1, n_tp):
            gather(ch, d).wait_recv()
        gather_own(ch).wait()

        @pl.when(has_up)
        def _():
            own_up(ch).start()

    def spread(ch):
        @pl.when(has_down)
        def _():
            own_up(ch).wait_recv()

        @pl.when(even & has_down)
        def _():
            st[ch] = jnp.where(side_k == 3, kvb[ch][2], kvb[ch][0])
            side(ch, st.at[ch]).start()

        @pl.when(even & jnp.logical_not(has_down))
        def _():
            side(ch, kvb[ch].at[0]).start()

        if ch % 2 == 0:
            @pl.when(odd & has_down)
            def _():
                side(ch, kvb[ch].at[2]).start()

            @pl.when(even & has_down)
            def _():
                side(ch, kvb[ch].at[0]).wait_recv()

                @pl.when(has_up)
                def _():
                    relay(ch).start()
        else:
            @pl.when(odd & has_down & has_up)
            def _():
                relay(ch).start()

            @pl.when(odd & (c >= 5))
            def _():
                relay(ch).wait_recv()
                st[ch] = jnp.where(side_k == 3, kvb[ch][3], kvb[ch][2])
                side(ch, st.at[ch]).start()

            @pl.when(odd & has_down & (c < 5))
            def _():
                side(ch, kvb[ch].at[2]).start()

    def arrive(ch):
        @pl.when(odd)
        def _():
            side(ch, kvb[ch].at[0]).wait_recv()

        if ch % 2 == 0:
            @pl.when(even & (c >= 4))
            def _():
                relay(ch).wait_recv()
        else:
            @pl.when(even & has_down)
            def _():
                side(ch, kvb[ch].at[0]).wait_recv()

    def to_side(ch):
        return copy(s1.at[ch], rp.at[ch], b_send.at[0, ch], b_recv.at[0, ch], partner, t)

    def three_down(ch):
        return copy(s1.at[ch], rd.at[ch], b_send.at[0, ch], b_recv.at[1, ch], c - 2, t)

    def two_down(ch):
        return copy(sc.at[ch], rc.at[ch], b_send.at[1, ch], b_recv.at[2, ch], c - 2, t)

    def pass_side(ch):
        return copy(se.at[ch], rp.at[ch], b_send.at[2, ch], b_recv.at[0, ch], partner, t)

    def pass_down(ch):
        return copy(se.at[ch], rd.at[ch], b_send.at[2, ch], b_recv.at[1, ch], c - 2, t)

    near_k = (ksel == 1) | (ksel == 3)

    def first_send(ch):
        part = prem[ch]
        wanted = near_k if ch % 2 else jnp.where(odd, near_k, ksel == 3)
        s1[ch] = jnp.where(wanted, part, jnp.zeros_like(part))

        @pl.when(odd)
        def _():
            to_side(ch).start()

        @pl.when(even & has_down)
        def _():
            (to_side if ch % 2 else three_down)(ch).start()

    def picked(ch, cond):
        part = prem[ch]
        return jnp.where(cond, part, jnp.zeros_like(part)).astype(jnp.float32)

    def even_mid(ch):
        @pl.when(even)
        def _():
            to_side(ch).wait_recv()
            got = rp[ch].astype(jnp.float32)

            @pl.when(has_down)
            def _():
                sc[ch] = (picked(ch, ksel == 2) + jnp.where(side_k == 3, got, 0.0)).astype(jnp.bfloat16)
                two_down(ch).start()

            acc[ch] = acc[ch] + jnp.where(side_k == 1, got, 0.0)

        if ch % 2 == 0:
            @pl.when(even & has_up)
            def _():
                three_down(ch).wait_recv()

            @pl.when(even & has_down & has_up)
            def _():
                se[ch] = (picked(ch, ksel == 1) + rd[ch].astype(jnp.float32)).astype(jnp.bfloat16)
                pass_side(ch).start()

            @pl.when(even & has_down & jnp.logical_not(has_up))
            def _():
                se[ch] = picked(ch, ksel == 1).astype(jnp.bfloat16)
                pass_side(ch).start()

    def odd_first(ch):
        if ch % 2:
            @pl.when(odd & has_down)
            def _():
                to_side(ch).wait_recv()

            @pl.when(odd & (c >= 5))
            def _():
                got = rp[ch]
                se[ch] = jnp.where(side_k == 3, got, jnp.zeros_like(got))
                pass_down(ch).start()

    def odd_mid(ch):
        if ch % 2 == 0:
            @pl.when(odd & has_down)
            def _():
                pass_side(ch).wait_recv()
                sc[ch] = (picked(ch, ksel == 2) + rp[ch].astype(jnp.float32)).astype(jnp.bfloat16)
                two_down(ch).start()
        else:
            def near_sum():
                got = rp[ch].astype(jnp.float32)
                return picked(ch, ksel == 2) + jnp.where(side_k == 1, got, 0.0)

            @pl.when(odd & has_down & has_up)
            def _():
                pass_down(ch).wait_recv()
                sc[ch] = (near_sum() + rd[ch].astype(jnp.float32)).astype(jnp.bfloat16)
                two_down(ch).start()

            @pl.when(odd & has_down & jnp.logical_not(has_up))
            def _():
                sc[ch] = near_sum().astype(jnp.bfloat16)
                two_down(ch).start()

    spread(0)
    spread(1)
    for g in range(groups):
        for ch in (2 * g, 2 * g + 1):
            arrive(ch)
        for h in range(g * per_group, (g + 1) * per_group):
            head_copy(0, h).wait()
            head_copy(1, h).wait()
        kcat[:half] = kvb[2 * g][0]
        kcat[half:] = kvb[2 * g][slot_of[0]]
        vcat[:half] = kvb[2 * g + 1][0]
        vcat[half:] = kvb[2 * g + 1][slot_of[1]]
        kt = jnp.transpose(kcat[...])
        base = g * per_group * toks

        def pair_step(p, carry):
            span = pl.ds(pl.multiple_of(p * 2 * toks, 2 * toks), 2 * toks)
            heads = pl.ds(pl.multiple_of(base + p * 2 * toks, 2 * toks), 2 * toks)
            nt = (((1,), (1,)), ((), ()))
            score = lax.dot_general(kcat[...], qs[heads], nt, preferred_element_type=jnp.float32)
            x = score * (scaling * LOG2E) + bias[...]
            top = jnp.maximum(jnp.max(x, axis=0, keepdims=True), 0.1 * NEG)
            e = jnp.exp2(x - top)
            inv = 1.0 / jnp.maximum(jnp.sum(e, axis=0, keepdims=True), 1.0)
            w = e * inv
            wt[:, span] = w.astype(jnp.bfloat16)
            gw = lax.dot_general(vcat[...], gs[heads], nt, preferred_element_type=jnp.float32)
            u = w * gw
            dot = jnp.sum(u, axis=0, keepdims=True)
            ds = (u - w * dot).astype(jnp.bfloat16)
            dst[:, span] = ds
            gqt = jnp.dot(kt, ds, preferred_element_type=jnp.float32) * scaling
            for i in range(2):
                cols = pl.ds(pl.multiple_of((g * per_group + 2 * p + i) * HD, HD), HD)
                gq[:, cols] = jnp.transpose(gqt[:, i * toks : (i + 1) * toks]).astype(jnp.bfloat16)
            return carry

        pairs = per_group // 2
        lax.fori_loop(0, pairs // 2, pair_step, 0)
        if g + 1 < groups:
            spread(2 * g + 2)
        if g > 0:
            even_mid(2 * g - 1)
        lax.fori_loop(pairs // 2, pairs, pair_step, 0)
        if g + 1 < groups:
            spread(2 * g + 3)
        if g > 0:
            odd_first(2 * g - 1)
            even_mid(2 * g - 2)
        own_rows = pl.ds(base, per_group * toks)
        for ch, (lhs, rhs) in ((2 * g, (dst, qs)), (2 * g + 1, (wt, gs))):
            scale = scaling if ch % 2 == 0 else 1.0
            total = jnp.dot(lhs[...], rhs[own_rows], preferred_element_type=jnp.float32) * scale
            acc[ch] = total[:half]
            prem[ch] = jnp.where(rem_ok, total[half:], 0.0).astype(jnp.bfloat16)
            first_send(ch)

    for ch in range(nch):
        if ch < nch - 2:
            odd_mid(ch)
    for ch in range(nch - 2, nch):
        even_mid(ch)
        odd_first(ch)
    for ch in range(nch - 2, nch):
        odd_mid(ch)

    def hand(ch, d):
        to = lax.rem(t + d, n_tp)
        return copy(
            fout.at[ch, pl.ds(pl.multiple_of(to * rows, rows), rows)], fin.at[d - 1, ch],
            z_send.at[d - 1, ch], z_recv.at[d - 1, ch], c, to,
        )

    for ch in range(nch):
        @pl.when(has_up)
        def _():
            two_down(ch).wait_recv()
            acc[ch] = acc[ch] + rc[ch].astype(jnp.float32)

        fout[ch] = acc[ch].astype(jnp.bfloat16)
        for d in range(1, n_tp):
            hand(ch, d).start()

    def put(ch, who, block):
        out = (gk, gv)[ch % 2]
        out[:, pl.ds(pl.multiple_of((who * groups + ch // 2) * HD, HD), HD)] = block

    for ch in range(nch):
        put(ch, t, acc[ch, pl.ds(pl.multiple_of(t * rows, rows), rows)])
    for ch in range(nch):
        for d in range(1, n_tp):
            hand(ch, d).wait_recv()
            put(ch, lax.rem(t + n_tp - d, n_tp), fin[d - 1, ch].astype(jnp.float32))

    for ch in range(nch):
        for d in range(1, n_tp):
            gather(ch, d).wait_send()
            hand(ch, d).wait_send()

        @pl.when(has_up)
        def _():
            own_up(ch).wait_send()

        @pl.when(even | has_down)
        def _():
            side(ch, kvb[ch].at[0]).wait_send()

        @pl.when((odd if ch % 2 else even) & has_down & has_up)
        def _():
            relay(ch).wait_send()

        @pl.when(odd | has_down)
        def _():
            to_side(ch).wait_send()

        @pl.when(has_down)
        def _():
            two_down(ch).wait_send()

        if ch % 2 == 0:
            @pl.when(even & has_down)
            def _():
                pass_side(ch).wait_send()
        else:
            @pl.when(odd & (c >= 5))
            def _():
                pass_down(ch).wait_send()


def on_device(n_ctx, n_tp, queries, keys, values, grad_out, readers, token_mask, image_len):
    rows, width = keys.shape
    groups = width // HD // n_tp
    toks = queries.shape[0]
    per_group = queries.shape[1] // HD // groups
    nch = 2 * groups
    half = rows * n_tp
    bf, f32 = jnp.bfloat16, jnp.float32
    vm = pl.BlockSpec(memory_space=pltpu.VMEM)
    hbm = pl.BlockSpec(memory_space=pltpu.HBM)
    sm = pl.BlockSpec(memory_space=pltpu.SMEM)
    dma = pltpu.SemaphoreType.DMA
    item = pltpu.VMEM((nch, half, HD), bf)
    return pl.pallas_call(
        functools.partial(kernel, n_ctx, n_tp, groups, per_group),
        out_shape=(
            jax.ShapeDtypeStruct(queries.shape, bf),
            jax.ShapeDtypeStruct(keys.shape, f32),
            jax.ShapeDtypeStruct(keys.shape, f32),
        ),
        in_specs=[sm, sm, hbm, hbm, hbm, hbm, vm],
        out_specs=(vm, vm, vm),
        scratch_shapes=[pltpu.VMEM((WIN, half, HD), bf)] * nch
        + [
            pltpu.VMEM((2 * half, 2 * toks), f32),
            pltpu.VMEM((2 * half, HD), bf),
            pltpu.VMEM((2 * half, HD), bf),
            pltpu.VMEM((groups * per_group * toks, HD), bf),
            pltpu.VMEM((groups * per_group * toks, HD), bf),
            pltpu.VMEM((2 * half, per_group * toks), bf),
            pltpu.VMEM((2 * half, per_group * toks), bf),
            pltpu.VMEM((nch, half, HD), f32),
            item, item, item, item, item, item, item,
            pltpu.VMEM((n_tp - 1, nch, rows, HD), bf),
            item, item,
            dma((2, groups * per_group)),
            dma((nch,)),
            dma((n_tp - 1, nch)), dma((n_tp - 1, nch)),
            dma((3, nch)), dma((3, nch)),
            dma((3, nch)), dma((3, nch)),
            dma((n_tp - 1, nch)), dma((n_tp - 1, nch)),
        ],
        compiler_params=pltpu.CompilerParams(
            collective_id=0, has_side_effects=True, vmem_limit_bytes=66_900_000
        ),
    )(readers.T, image_len, queries, grad_out, keys, values, token_mask.T)


def solution(mesh):
    n_ctx, n_tp = mesh.shape["ctx"], mesh.shape["tp"]
    return jax.shard_map(
        functools.partial(on_device, n_ctx, n_tp),
        mesh=mesh,
        in_specs=(
            P("ctx", "tp"),
            P(("ctx", "tp"), None),
            P(("ctx", "tp"), None),
            P("ctx", "tp"),
            P(),
            P("ctx", None),
            P(),
        ),
        out_specs=(P("ctx", "tp"), P(("ctx", "tp"), None), P(("ctx", "tp"), None)),
        check_vma=False,
    )
```

time: 71.2 us -> 75.4 us (1.059)
  Pallas kernels: 63 us -> 70.6 us
  local copies, waits for them, and re-layouts: 7.14 us -> 3.97 us
    pallas_call x1, Pallas kernels: 63 us -> 70.6 us  [on_device(): pl.pallas_call(functools.partial(kernel, n_ctx, n_tp, groups, per_group),...]
    unnamed x16 -> x7, local copies, waits for them, and re-layouts: 7.14 us -> 3.97 us
where the time goes in v1:
time: 75.4 us; the launch traced here: 75.2 us
  Pallas kernels  70.6 us (94%)
  local copies, waits for them, and re-layouts  3.97 us (5%)
    pallas_call x1, Pallas kernels, on_device(): pl.pallas_call(functools.partial(kernel, n_ctx, n_tp, groups, per_group),...  70.6 us
    unnamed x7, local copies, waits for them, and re-layouts  3.97 us

profile of v1, /device:TPU:15, one launch (start us, length us, event | category | flops | bytes accessed | tf_op | source)
XLA Modules:
  0.0 75.2 jit_solution(7849300555106946547)
XLA Ops:
  0.6 70.6 %shard_map.94 = (bf16[128,2048]{1,0:T(8,128)(2,1)}, f32[128,1024]{1,0:T(8,128)}, f32[128,1024]{1,0:T(8,128)}) custom-call(s32[4,8]{1,0:T(4,128)} %bitcast.2, s32[16]{0:T(128)} %image_len.1, bf16[128,2048]{1,0:T(8,128)(2,1)} %q.1, bf16[128,2048]{1,0:T(8,128)(2,1)} %go.1, bf16[128,1024]{1,0:T(8,128)(2,1)} %k.1, bf16[128,1024]{1,0:T(8,128)(2,1)} %v.1, ...), custom_call_target="tpu_custom_call" | custom-call | tf_op jit(solution)/shard_map/pallas_call | solution.py:438
  71.2 0.0 copy-start.1
  71.2 1.9 %copy.13 = bf16[128,2048]{1,0:T(8,128)(2,1)} copy(bf16[128,2048]{1,0:T(8,128)(2,1)} %get-tuple-element.6) | data formatting | bytes 1048576
  73.2 0.0 copy-done.1
  73.2 0.0 copy-start
  73.2 0.8 %copy.14 = f32[128,1024]{1,0:T(8,128)} copy(f32[128,1024]{1,0:T(8,128)S(1)} %copy-done.1) | data formatting | bytes 1048576
  74.0 0.4 copy-done
  74.4 0.8 %copy.15 = f32[128,1024]{1,0:T(8,128)} copy(f32[128,1024]{1,0:T(8,128)S(1)} %copy-done) | data formatting | bytes 1048576
Async XLA Ops:
  71.2 2.0 %copy-start.1 = (f32[128,1024]{1,0:T(8,128)S(1)}, f32[128,1024]{1,0:T(8,128)}, u32[]{:S(2)}) copy-start(f32[128,1024]{1,0:T(8,128)} %get-tuple-element.7) | copy-start | bytes 1572868
  73.2 1.2 %copy-start = (f32[128,1024]{1,0:T(8,128)S(1)}, f32[128,1024]{1,0:T(8,128)}, u32[]{:S(2)}) copy-start(f32[128,1024]{1,0:T(8,128)} %get-tuple-element.8) | copy-start | bytes 1572868

commit v2 on v0

--- a/solution.py
+++ b/solution.py
@@ -90,13 +90,13 @@
             gather(ch, d).start()
         gather_own(ch).start()
 
-    rem_id = readers[c, IMG_DEV]
+    rem_id = readers[IMG_DEV, c]
     rem_ok = rem_id >= 0
     rem_owner = jnp.maximum(rem_id, 0) // IMG_DEV
     ksel = jnp.where(rem_ok, c - rem_owner, 0)
     kload = jnp.clip(ksel, 0, WIN - 1)
     up_row = jnp.minimum(c + 1, n_ctx - 1)
-    up_id = readers[up_row, IMG_DEV]
+    up_id = readers[IMG_DEV, up_row]
     up_k = jnp.where(up_id >= 0, c + 1 - jnp.maximum(up_id, 0) // IMG_DEV, 0)
     for b in range(SLOTS):
         run = (b // IMG_DEV) * IMG_DEV
@@ -105,7 +105,7 @@
         length = image_len[image]
         if b >= IMG_DEV:
             length = jnp.where(rem_ok, length, 0)
-        mask = jnp.where(readers[c, run] == image, tm[run : run + 1], tm[run + 1 : run + 2])
+        mask = jnp.where(readers[run, c] == image, tm[run : run + 1], tm[run + 1 : run + 2])
         live = jnp.where(mask == 1, length, 0)
         place = lax.broadcasted_iota(jnp.int32, (itok, toks), 0)
         block = jnp.where(place < live, 0.0, NEG).astype(jnp.float32)
@@ -140,7 +140,7 @@
         def _():
             own_next(ch).start()
 
-    for ch in range(nch):
+    def near(ch):
         @pl.when(has_down)
         def _():
             own_up(ch).wait_recv()
@@ -153,6 +153,7 @@
             def _():
                 two_back(ch).start()
 
+    def far(ch):
         @pl.when(even & has_down)
         def _():
             two_back(ch).wait_recv()
@@ -164,6 +165,12 @@
         @pl.when(odd)
         def _():
             own_next(ch).wait_recv()
+
+    near(0)
+    for ch in range(1, nch):
+        near(ch)
+        far(ch - 1)
+    far(nch - 1)
 
     def arrive(ch):
         @pl.when(odd & has_down)
@@ -385,7 +392,7 @@
         compiler_params=pltpu.CompilerParams(
             collective_id=0, has_side_effects=True, vmem_limit_bytes=50 * 1024 * 1024
         ),
-    )(readers, image_len, queries, grad_out, keys, values, token_mask.T)
+    )(readers.T, image_len, queries, grad_out, keys, values, token_mask.T)
 
 
 def solution(mesh):

time: 71.2 us -> 71.8 us (level)
    unnamed x16 -> x17, local copies, waits for them, and re-layouts: 7.14 us -> 7.71 us
where the time goes in v2:
time: 71.8 us; the launch traced here: 71.4 us
  Pallas kernels  63 us (88%)
  local copies, waits for them, and re-layouts  7.71 us (11%)
    pallas_call x1, Pallas kernels, on_device(): pl.pallas_call(functools.partial(kernel, n_ctx, n_tp, groups, per_group),...  63 us
    unnamed x17, local copies, waits for them, and re-layouts  7.71 us

profile of v2, /device:TPU:15, one launch (start us, length us, event | category | flops | bytes accessed | tf_op | source)
XLA Modules:
  0.0 71.4 jit_solution(1812200414616090036)
XLA Ops:
  0.6 0.0 copy-start.4
  0.6 0.0 copy-start.6
  0.7 0.7 copy-done.4
  1.3 0.0 copy-done.6
  1.3 0.0 copy-start
  1.3 1.0 %copy-done = bf16[128,2048]{1,0:T(8,128)(2,1)S(1)} copy-done((bf16[128,2048]{1,0:T(8,128)(2,1)S(1)}, bf16[128,2048]{1,0:T(8,128)(2,1)}, u32[]{:S(2)}) %copy-start) | copy-done | bytes 524312
  2.4 0.0 copy-start.1
  2.4 1.0 %copy-done.1 = bf16[128,2048]{1,0:T(8,128)(2,1)S(1)} copy-done((bf16[128,2048]{1,0:T(8,128)(2,1)S(1)}, bf16[128,2048]{1,0:T(8,128)(2,1)}, u32[]{:S(2)}) %copy-start.1) | copy-done | bytes 524312
  3.4 0.0 copy-start.2
  3.4 0.9 %copy-done.2 = bf16[128,1024]{1,0:T(8,128)(2,1)S(1)} copy-done((bf16[128,1024]{1,0:T(8,128)(2,1)S(1)}, bf16[128,1024]{1,0:T(8,128)(2,1)}, u32[]{:S(2)}) %copy-start.2) | copy-done | bytes 262168
  4.4 0.0 copy-start.3
  4.4 0.9 %copy-done.3 = bf16[128,1024]{1,0:T(8,128)(2,1)S(1)} copy-done((bf16[128,1024]{1,0:T(8,128)(2,1)S(1)}, bf16[128,1024]{1,0:T(8,128)(2,1)}, u32[]{:S(2)}) %copy-start.3) | copy-done | bytes 262168
  5.3 0.0 copy-start.5
  5.3 0.7 copy-done.5
  6.0 63.0 %shard_map.94 = (bf16[128,2048]{1,0:T(8,128)(2,1)S(1)}, f32[128,1024]{1,0:T(8,128)S(1)}, f32[128,1024]{1,0:T(8,128)S(1)}) custom-call(s32[4,8]{1,0:T(4,128)S(1)} %bitcast.2, s32[16]{0:T(128)S(1)} %copy-done.6, bf16[128,2048]{1,0:T(8,128)(2,1)S(1)} %copy-done, bf16[128,2048]{1,0:T(8,128)(2,1)S(1)} %copy-done.1, bf16[128,1024]{1,0:T(8,128)(2,1)S(1)} %copy-done.2, ...), custom_call_target="tpu_custom_call" | custom-call | tf_op jit(solution)/shard_map/pallas_call | solution.py:364
  69.0 0.8 %copy.13 = bf16[128,2048]{1,0:T(8,128)(2,1)} copy(bf16[128,2048]{1,0:T(8,128)(2,1)S(1)} %get-tuple-element.6) | data formatting | bytes 1048576
  69.8 0.8 %copy.14 = f32[128,1024]{1,0:T(8,128)} copy(f32[128,1024]{1,0:T(8,128)S(1)} %get-tuple-element.7) | data formatting | bytes 1048576
  70.6 0.8 %copy.15 = f32[128,1024]{1,0:T(8,128)} copy(f32[128,1024]{1,0:T(8,128)S(1)} %get-tuple-element.8) | data formatting | bytes 1048576
Async XLA Ops:
  0.6 0.7 copy-start.4
  0.6 0.7 copy-start.6
  1.3 1.0 %copy-start = (bf16[128,2048]{1,0:T(8,128)(2,1)S(1)}, bf16[128,2048]{1,0:T(8,128)(2,1)}, u32[]{:S(2)}) copy-start(bf16[128,2048]{1,0:T(8,128)(2,1)} %q.1) | copy-start | bytes 1572868
  2.4 1.0 %copy-start.1 = (bf16[128,2048]{1,0:T(8,128)(2,1)S(1)}, bf16[128,2048]{1,0:T(8,128)(2,1)}, u32[]{:S(2)}) copy-start(bf16[128,2048]{1,0:T(8,128)(2,1)} %go.1) | copy-start | bytes 1572868
  3.4 0.9 %copy-start.2 = (bf16[128,1024]{1,0:T(8,128)(2,1)S(1)}, bf16[128,1024]{1,0:T(8,128)(2,1)}, u32[]{:S(2)}) copy-start(bf16[128,1024]{1,0:T(8,128)(2,1)} %k.1) | copy-start | bytes 786436
  4.4 0.9 %copy-start.3 = (bf16[128,1024]{1,0:T(8,128)(2,1)S(1)}, bf16[128,1024]{1,0:T(8,128)(2,1)}, u32[]{:S(2)}) copy-start(bf16[128,1024]{1,0:T(8,128)(2,1)} %v.1) | copy-start | bytes 786436
  5.3 0.7 copy-start.5
